TPU v7x, 32 devices: a whole 2x2x4 slice. The times are simulated.
32 devices in a mesh: gx: 4 (over y, core), gy: 2 (over x), ch: 4 (over z).
Axes of the slice: x: 2, y: 2, z: 4, core: 2. Of those that a mesh axis runs over, the one named last changes fastest.
Arguments:
- density: bfloat16 [4, 32, 128, 128], P('gx', 'gy', 'ch'), may hold values from -6 to 6
- first_kernel: bfloat16 [3, 3, 3, 128, 128], P(None, None, None, 'ch'), may hold values from -0.109375 to 0.109375
- first_bias: float32 [128], P('ch'), may hold values from -3 to 3
- second_kernel: bfloat16 [3, 3, 3, 128, 128], P(None, None, None, 'ch'), may hold values from -0.109375 to 0.109375
- second_bias: float32 [128], P('ch'), may hold values from -3 to 3
Outputs:
- features: bfloat16 [4, 32, 128, 128], P('gx', 'gy', 'ch')
All inputs are finite; a program needn't handle non-finite values.
Results may differ from a plain program's by a relative error of at most 0.0045.
Values may be sent and summed in bfloat16 or wider, within the bound.
No kernel may reach another device: no remote copies, remote signals or barrier semaphores. Data moves between devices by JAX's collectives and lax.ppermute only.
A program may use at most 64 MiB of HBM per device.

v0:
```python
import jax
import jax.numpy as jnp
from jax import lax
from jax.sharding import PartitionSpec as P


def with_halo(block, sides, width):
    for axis, dim in sides:
        count = lax.axis_size(axis)
        forward = [(i, i + 1) for i in range(count - 1)]
        backward = [(target, source) for source, target in forward]
        low = lax.ppermute(
            lax.slice_in_dim(block, block.shape[dim] - width, None, axis=dim), axis, forward
        )
        high = lax.ppermute(lax.slice_in_dim(block, 0, width, axis=dim), axis, backward)
        block = jnp.concatenate([low, block, high], axis=dim)
    return block


def conv_taps(padded, kernel):
    result = lax.conv_general_dilated(
        padded[None],
        kernel,
        (1, 1, 1),
        "VALID",
        dimension_numbers=("NHWCD", "HWDOI", "NHWCD"),
        preferred_element_type=jnp.float32,
    )
    return result[0]


def finish(total, bias):
    return jnp.maximum(total + bias.reshape(1, 1, -1, 1), 0.0).astype(jnp.bfloat16)


def pad_depth(field):
    return jnp.pad(field, ((0, 0), (0, 0), (0, 0), (1, 1)))


def layer_channels(field, kernel, bias):
    whole = lax.all_gather(field, "ch", axis=2, tiled=True)
    padded = with_halo(pad_depth(whole), (("gx", 0), ("gy", 1)), 1)
    total = conv_taps(padded, kernel)
    return finish(total, bias)


def per_device(density, first_kernel, first_bias, second_kernel, second_bias):
    hidden = layer_channels(density, first_kernel, first_bias)
    return layer_channels(hidden, second_kernel, second_bias)


def solution(mesh):
    placed = (
        P("gx", "gy", "ch", None),
        P(None, None, None, "ch", None),
        P("ch"),
        P(None, None, None, "ch", None),
        P("ch"),
    )
    return jax.shard_map(
        per_device, mesh=mesh, in_specs=placed, out_specs=P("gx", "gy", "ch", None), check_vma=False
    )
```

profile of v0, /device:TPU:12, one launch (start us, length us, event | category | flops | bytes accessed | tf_op | source)
XLA Modules:
  0.0 126.0 jit_solution(12742077173878891672)
XLA Ops:
  0.0 1.0 copy.78
  1.0 16.5 %all_gather.6 = bf16[1,16,128,128]{3,1,0,2:T(8,128)(2,1)S(1)} all-gather(bf16[1,16,32,128]{3,1,0,2:T(8,128)(2,1)S(1)} %copy.78), channel_id=1, replica_groups=mesh['gx'=4,'gy'=2,'ch'=4] {'ch'}, dimensions={2}, use_global_device_ids=true | all-gather | bytes 655360 | tf_op jit(solution)/shard_map/all_gather | solution.py:41
  17.5 0.4 pad.7
  17.9 1.2 copy.79
  19.1 1.9 %collective-permute-start.1 = (bf16[1,16,128,130]{2,1,3,0:T(8,128)(2,1)S(1)}, bf16[1,16,128,130]{2,1,3,0:T(8,128)(2,1)S(1)}, u32[]{:S(2)}, u32[]{:S(2)}) collective-permute-start(bf16[1,16,128,130]{2,1,3,0:T(8,128)(2,1)S(1)} %copy.79), channel_id=1, source_target_pairs={{8,0},{16,8},{24,16},{9,1},{17,9},{25,17},{10,2},{18,10},{26,18},{... | collective-permute-start | bytes 1597448 | tf_op jit(solution)/shard_map/ppermute | solution.py:15
  21.0 2.4 %collective-permute-start = (bf16[1,16,128,130]{2,1,3,0:T(8,128)(2,1)S(1)}, bf16[1,16,128,130]{2,1,3,0:T(8,128)(2,1)S(1)}, u32[]{:S(2)}, u32[]{:S(2)}) collective-permute-start(bf16[1,16,128,130]{2,1,3,0:T(8,128)(2,1)S(1)} %copy.79), channel_id=1, source_target_pairs={{0,8},{8,16},{16,24},{1,9},{9,17},{17,25},{2,10},{10,18},{18,26},{... | collective-permute-start | bytes 1597448 | tf_op jit(solution)/shard_map/ppermute | solution.py:12
  23.4 4.3 %collective-permute-done.1 = bf16[1,16,128,130]{2,1,3,0:T(8,128)(2,1)S(1)} collective-permute-done((bf16[1,16,128,130]{2,1,3,0:T(8,128)(2,1)S(1)}, bf16[1,16,128,130]{2,1,3,0:T(8,128)(2,1)S(1)}, u32[]{:S(2)}, u32[]{:S(2)}) %collective-permute-start.1) | collective-permute-done | bytes 532512 | tf_op jit(solution)/shard_map/ppermute | solution.py:15
  27.8 1.8 %copy.82 = bf16[1,16,128,130]{3,1,0,2:T(8,128)(2,1)} copy(bf16[1,16,128,130]{2,1,3,0:T(8,128)(2,1)S(1)} %collective-permute-done.1) | data formatting | bytes 1064960 | tf_op jit(solution)/shard_map/ppermute | solution.py:15
  29.6 2.0 %collective-permute-done = bf16[1,16,128,130]{2,1,3,0:T(8,128)(2,1)S(1)} collective-permute-done((bf16[1,16,128,130]{2,1,3,0:T(8,128)(2,1)S(1)}, bf16[1,16,128,130]{2,1,3,0:T(8,128)(2,1)S(1)}, u32[]{:S(2)}, u32[]{:S(2)}) %collective-permute-start) | collective-permute-done | bytes 532512 | tf_op jit(solution)/shard_map/ppermute | solution.py:12
  31.6 1.8 %copy.81 = bf16[1,16,128,130]{3,1,0,2:T(8,128)(2,1)} copy(bf16[1,16,128,130]{2,1,3,0:T(8,128)(2,1)S(1)} %collective-permute-done) | data formatting | bytes 1064960 | tf_op jit(solution)/shard_map/ppermute | solution.py:12
  33.4 2.4 %pad_maximum_fusion = bf16[3,16,128,130]{3,1,0,2:T(8,128)(2,1)S(1)} fusion(bf16[1,16,128,130]{3,1,0,2:T(8,128)(2,1)} %copy.82, bf16[1,16,128,130]{3,1,0,2:T(8,128)(2,1)} %copy-done.1, bf16[1,16,128,130]{3,1,0,2:T(8,128)(2,1)} %copy.81), kind=kLoop, calls=%fused_computation.3 | loop fusion | flops 1597440 | bytes 3194880 | tf_op jit(solution)/shard_map/concatenate | solution.py:16
  35.9 1.5 %fusion.35 = (bf16[3,1,128,130]{3,1,0,2:T(2,128)(2,1)}, bf16[3,1,128,130]{3,1,0,2:T(2,128)(2,1)}) fusion(bf16[3,16,128,130]{3,1,0,2:T(8,128)(2,1)S(1)} %pad_maximum_fusion), kind=kLoop, calls=%fused_computation.36 | loop fusion | bytes 399360 | tf_op jit(solution)/shard_map/slice | solution.py:13
  37.3 1.2 copy.83
  38.6 1.8 %copy.84 = bf16[3,1,128,130]{2,3,1,0:T(8,128)(2,1)} copy(bf16[3,1,128,130]{3,1,0,2:T(2,128)(2,1)} %get-tuple-element.8) | data formatting | bytes 199680 | tf_op jit(solution)/shard_map/slice | solution.py:15
  40.4 1.3 %collective-permute-start.3 = (bf16[3,1,128,130]{2,3,1,0:T(8,128)(2,1)}, bf16[3,1,128,130]{2,3,1,0:T(8,128)(2,1)}, u32[]{:S(2)}, u32[]{:S(2)}) collective-permute-start(bf16[3,1,128,130]{2,3,1,0:T(8,128)(2,1)} %copy.84), channel_id=1, source_target_pairs={{4,0},{5,1},{6,2},{7,3},{12,8},{13,9},{14,10},{15,11},{20,16},{21,... | collective-permute-start | bytes 299528 | tf_op jit(solution)/shard_map/ppermute | solution.py:15
  41.6 5.8 %collective-permute-start.2 = (bf16[3,1,128,130]{2,3,1,0:T(8,128)(2,1)S(1)}, bf16[3,1,128,130]{2,3,1,0:T(8,128)(2,1)}, u32[]{:S(2)}, u32[]{:S(2)}) collective-permute-start(bf16[3,1,128,130]{2,3,1,0:T(8,128)(2,1)S(1)} %copy.83), channel_id=1, source_target_pairs={{0,4},{1,5},{2,6},{3,7},{8,12},{9,13},{10,14},{11,15},{16,20},{17,... | collective-permute-start | bytes 299528 | tf_op jit(solution)/shard_map/ppermute | solution.py:12
  47.5 3.2 %copy.85 = bf16[3,16,128,130]{2,3,1,0:T(8,128)(2,1)} copy(bf16[3,16,128,130]{3,1,0,2:T(8,128)(2,1)S(1)} %pad_maximum_fusion) | data formatting | bytes 3194880 | tf_op jit(solution)/shard_map/concatenate | solution.py:16
  50.7 1.7 %maximum_bitcast_fusion = bf16[3,18,128,1,130]{2,4,1,0,3:T(8,128)(2,1)S(1)} fusion(bf16[3,1,128,130]{2,3,1,0:T(8,128)(2,1)} %collective-permute-done.3, bf16[3,16,128,130]{2,3,1,0:T(8,128)(2,1)} %copy.85, bf16[3,1,128,130]{2,3,1,0:T(8,128)(2,1)} %collective-permute-done.2), kind=kLoop, calls=%fused_computation.17 | loop fusion | flops 1797120 | bytes 3594240 | tf_op jit(solution)/shard_map/broadcast_in_dim | solution.py:22
  52.4 1.4 %pad.9 = bf16[3,18,128,1,136]{2,4,1,0,3:T(8,128)(2,1)} pad(bf16[3,18,128,1,130]{2,4,1,0,3:T(8,128)(2,1)S(1)} %maximum_bitcast_fusion, bf16[]{:T(256)} %constant.1.clone.1), padding=0_0x0_0x0_0x0_0x0_6 | pad | bytes 3677186 | tf_op jit(solution)/shard_map/broadcast_in_dim | solution.py:22
  53.8 3.3 %reshape.50 = bf16[3,18,128,1,8,17]{2,5,4,1,0,3:T(8,128)(2,1)S(1)} reshape(bf16[3,18,128,1,136]{2,4,1,0,3:T(8,128)(2,1)} %pad.9) | data formatting | bytes 3760128 | tf_op jit(solution)/shard_map/conv_general_dilated | solution.py:21
  57.1 0.0 copy-start.6
  57.2 0.3 copy.87
  57.4 0.1 slice.22
  57.5 0.3 copy-done.6
  57.8 4.2 %fusion.19 = f32[1,16,8,17,32]{4,2,3,1,0:T(8,128)S(1)} fusion(bf16[3,3,3,32,128]{4,3,2,1,0:T(8,128)(2,1)S(1)} %copy-done, bf16[3,18,128,1,7,2]{2,4,5,1,0,3:T(8,128)(2,1)S(1)} %slice.22, bf16[3,18,128,1,8,17]{2,4,5,1,0,3:T(8,128)(2,1)S(1)} %copy.87, pred[8,17]{0,1:T(8,128)(4,1)S(1)} %copy-done.6), kind=kOutput, calls=%fused_computation.20 | convolution fusion | flops 487669760 | bytes 2573448 | tf_op jit(solution)/shard_map/conv_general_dilated | solution.py:21
  62.1 0.2 copy.88
  62.3 0.0 copy-start.3
  62.3 0.1 slice.23
  62.4 0.4 copy.102
  62.8 0.2 copy-done.3
  63.0 0.1 fusion.27
  63.1 0.1 copy.90
  63.1 15.0 %all_gather.7 = bf16[1,16,128,128]{3,1,0,2:T(8,128)(2,1)S(1)} all-gather(bf16[1,16,32,128]{3,1,0,2:T(8,128)(2,1)S(1)} %copy.90), channel_id=1, replica_groups=mesh['gx'=4,'gy'=2,'ch'=4] {'ch'}, dimensions={2}, use_global_device_ids=true | all-gather | bytes 655360 | tf_op jit(solution)/shard_map/all_gather | solution.py:41
  78.1 0.4 pad.8
  78.5 1.2 copy.91
  79.7 1.9 %collective-permute-start.5 = (bf16[1,16,128,130]{2,1,3,0:T(8,128)(2,1)S(1)}, bf16[1,16,128,130]{2,1,3,0:T(8,128)(2,1)S(1)}, u32[]{:S(2)}, u32[]{:S(2)}) collective-permute-start(bf16[1,16,128,130]{2,1,3,0:T(8,128)(2,1)S(1)} %copy.91), channel_id=1, source_target_pairs={{8,0},{16,8},{24,16},{9,1},{17,9},{25,17},{10,2},{18,10},{26,18},{... | collective-permute-start | bytes 1597448 | tf_op jit(solution)/shard_map/ppermute | solution.py:15
  81.6 2.6 %collective-permute-start.4 = (bf16[1,16,128,130]{2,1,3,0:T(8,128)(2,1)S(1)}, bf16[1,16,128,130]{2,1,3,0:T(8,128)(2,1)S(1)}, u32[]{:S(2)}, u32[]{:S(2)}) collective-permute-start(bf16[1,16,128,130]{2,1,3,0:T(8,128)(2,1)S(1)} %copy.91), channel_id=1, source_target_pairs={{0,8},{8,16},{16,24},{1,9},{9,17},{17,25},{2,10},{10,18},{18,26},{... | collective-permute-start | bytes 1597448 | tf_op jit(solution)/shard_map/ppermute | solution.py:12
  84.2 4.1 %collective-permute-done.5 = bf16[1,16,128,130]{2,1,3,0:T(8,128)(2,1)S(1)} collective-permute-done((bf16[1,16,128,130]{2,1,3,0:T(8,128)(2,1)S(1)}, bf16[1,16,128,130]{2,1,3,0:T(8,128)(2,1)S(1)}, u32[]{:S(2)}, u32[]{:S(2)}) %collective-permute-start.5) | collective-permute-done | bytes 532512 | tf_op jit(solution)/shard_map/ppermute | solution.py:15
  88.4 1.8 %copy.94 = bf16[1,16,128,130]{3,1,0,2:T(8,128)(2,1)} copy(bf16[1,16,128,130]{2,1,3,0:T(8,128)(2,1)S(1)} %collective-permute-done.5) | data formatting | bytes 1064960 | tf_op jit(solution)/shard_map/ppermute | solution.py:15
  90.2 2.0 %collective-permute-done.4 = bf16[1,16,128,130]{2,1,3,0:T(8,128)(2,1)S(1)} collective-permute-done((bf16[1,16,128,130]{2,1,3,0:T(8,128)(2,1)S(1)}, bf16[1,16,128,130]{2,1,3,0:T(8,128)(2,1)S(1)}, u32[]{:S(2)}, u32[]{:S(2)}) %collective-permute-start.4) | collective-permute-done | bytes 532512 | tf_op jit(solution)/shard_map/ppermute | solution.py:12
  92.2 1.8 %copy.93 = bf16[1,16,128,130]{3,1,0,2:T(8,128)(2,1)} copy(bf16[1,16,128,130]{2,1,3,0:T(8,128)(2,1)S(1)} %collective-permute-done.4) | data formatting | bytes 1064960 | tf_op jit(solution)/shard_map/ppermute | solution.py:12
  94.0 2.4 %pad_maximum_fusion.1 = bf16[3,16,128,130]{3,1,0,2:T(8,128)(2,1)S(1)} fusion(bf16[1,16,128,130]{3,1,0,2:T(8,128)(2,1)} %copy.94, bf16[1,16,128,130]{3,1,0,2:T(8,128)(2,1)} %copy-done.2, bf16[1,16,128,130]{3,1,0,2:T(8,128)(2,1)} %copy.93), kind=kLoop, calls=%fused_computation.4 | loop fusion | flops 1597440 | bytes 3194880 | tf_op jit(solution)/shard_map/concatenate | solution.py:16
  96.5 1.5 %fusion.34 = (bf16[3,1,128,130]{3,1,0,2:T(2,128)(2,1)}, bf16[3,1,128,130]{3,1,0,2:T(2,128)(2,1)}) fusion(bf16[3,16,128,130]{3,1,0,2:T(8,128)(2,1)S(1)} %pad_maximum_fusion.1), kind=kLoop, calls=%fused_computation.35 | loop fusion | bytes 399360 | tf_op jit(solution)/shard_map/slice | solution.py:13
  98.0 3.6 %collective-permute-start.6 = (bf16[3,1,128,130]{3,1,0,2:T(2,128)(2,1)}, bf16[3,1,128,130]{3,1,0,2:T(2,128)(2,1)}, u32[]{:S(2)}, u32[]{:S(2)}) collective-permute-start(bf16[3,1,128,130]{3,1,0,2:T(2,128)(2,1)} %get-tuple-element.5), channel_id=1, source_target_pairs={{0,4},{1,5},{2,6},{3,7},{8,12},{9,13},{10,14},{11,15},{16,20},{17,... | collective-permute-start | bytes 299528 | tf_op jit(solution)/shard_map/ppermute | solution.py:12
  101.6 1.3 %collective-permute-start.7 = (bf16[3,1,128,130]{3,1,0,2:T(2,128)(2,1)}, bf16[3,1,128,130]{3,1,0,2:T(2,128)(2,1)}, u32[]{:S(2)}, u32[]{:S(2)}) collective-permute-start(bf16[3,1,128,130]{3,1,0,2:T(2,128)(2,1)} %get-tuple-element.6), channel_id=1, source_target_pairs={{4,0},{5,1},{6,2},{7,3},{12,8},{13,9},{14,10},{15,11},{20,16},{21,... | collective-permute-start | bytes 299528 | tf_op jit(solution)/shard_map/ppermute | solution.py:15
  102.9 3.2 %copy.96 = bf16[3,16,128,130]{2,3,1,0:T(8,128)(2,1)} copy(bf16[3,16,128,130]{3,1,0,2:T(8,128)(2,1)S(1)} %pad_maximum_fusion.1) | data formatting | bytes 3194880 | tf_op jit(solution)/shard_map/concatenate | solution.py:16
  106.0 0.4 collective-permute-done.6
  106.4 1.2 copy.95
  107.7 3.9 %collective-permute-done.7 = bf16[3,1,128,130]{3,1,0,2:T(2,128)(2,1)} collective-permute-done((bf16[3,1,128,130]{3,1,0,2:T(2,128)(2,1)}, bf16[3,1,128,130]{3,1,0,2:T(2,128)(2,1)}, u32[]{:S(2)}, u32[]{:S(2)}) %collective-permute-start.7) | collective-permute-done | bytes 99872 | tf_op jit(solution)/shard_map/ppermute | solution.py:15
  111.5 1.2 copy.97
  112.8 1.7 %maximum_bitcast_fusion.1 = bf16[3,18,128,1,130]{2,4,1,0,3:T(8,128)(2,1)S(1)} fusion(bf16[3,1,128,130]{2,3,1,0:T(8,128)(2,1)S(1)} %copy.97, bf16[3,16,128,130]{2,3,1,0:T(8,128)(2,1)} %copy.96, bf16[3,1,128,130]{2,3,1,0:T(8,128)(2,1)S(1)} %copy.95), kind=kLoop, calls=%fused_computation.18 | loop fusion | flops 1797120 | bytes 3594240 | tf_op jit(solution)/shard_map/broadcast_in_dim | solution.py:22
  114.5 1.4 %pad.11 = bf16[3,18,128,1,136]{2,4,1,0,3:T(8,128)(2,1)} pad(bf16[3,18,128,1,130]{2,4,1,0,3:T(8,128)(2,1)S(1)} %maximum_bitcast_fusion.1, bf16[]{:T(256)} %constant.1.clone.1), padding=0_0x0_0x0_0x0_0x0_6 | pad | bytes 3677186 | tf_op jit(solution)/shard_map/broadcast_in_dim | solution.py:22
  115.9 3.3 %reshape.57 = bf16[3,18,128,1,8,17]{2,5,4,1,0,3:T(8,128)(2,1)S(1)} reshape(bf16[3,18,128,1,136]{2,4,1,0,3:T(8,128)(2,1)} %pad.11) | data formatting | bytes 3760128 | tf_op jit(solution)/shard_map/conv_general_dilated | solution.py:21
  119.2 0.0 copy-start.5
  119.2 0.3 copy.99
  119.5 0.1 slice.26
  119.6 0.6 copy-done.5
  120.2 4.2 %fusion.16 = f32[1,16,8,17,32]{4,2,3,1,0:T(8,128)S(1)} fusion(bf16[3,3,3,32,128]{4,3,2,1,0:T(8,128)(2,1)S(1)} %copy-done.5, bf16[3,18,128,1,7,2]{2,4,5,1,0,3:T(8,128)(2,1)S(1)} %slice.26, bf16[3,18,128,1,8,17]{2,4,5,1,0,3:T(8,128)(2,1)S(1)} %copy.99, pred[8,17]{0,1:T(8,128)(4,1)S(1)} %copy-done.6), kind=kOutput, calls=%fused_computation.19 | convolution fusion | flops 487669760 | bytes 2573448 | tf_op jit(solution)/shard_map/conv_general_dilated | solution.py:21
  124.4 0.2 copy.100
  124.6 0.0 copy-start.4
  124.6 0.1 slice.27
  124.7 0.4 copy.103
  125.1 0.2 copy-done.4
  125.3 0.8 fusion.25
  (8 shorter events, 0.0 us)
Async XLA Ops:
  0.0 57.5 %copy-start = (bf16[3,3,3,32,128]{4,3,2,1,0:T(8,128)(2,1)S(1)}, bf16[3,3,3,32,128]{4,3,2,1,0:T(8,128)(2,1)}, u32[]{:S(2)}) copy-start(bf16[3,3,3,32,128]{4,3,2,1,0:T(8,128)(2,1)} %param.6) | copy-start | bytes 663556
  17.9 13.7 %copy-start.1 = (bf16[1,16,128,130]{3,1,0,2:T(8,128)(2,1)}, bf16[1,16,128,130]{3,1,0,2:T(8,128)(2,1)S(1)}, u32[]{:S(2)}) copy-start(bf16[1,16,128,130]{3,1,0,2:T(8,128)(2,1)S(1)} %pad.7) | copy-start | bytes 1597444
  19.1 8.7 %collective-permute-start.1 = (bf16[1,16,128,130]{2,1,3,0:T(8,128)(2,1)S(1)}, bf16[1,16,128,130]{2,1,3,0:T(8,128)(2,1)S(1)}, u32[]{:S(2)}, u32[]{:S(2)}) collective-permute-start(bf16[1,16,128,130]{2,1,3,0:T(8,128)(2,1)S(1)} %copy.79), channel_id=1, source_target_pairs={{8,0},{16,8},{24,16},{9,1},{17,9},{25,17},{10,2},{18,10},{26,18},{... | collective-permute-start | bytes 1597448 | tf_op jit(solution)/shard_map/ppermute | solution.py:15
  21.0 10.6 %collective-permute-start = (bf16[1,16,128,130]{2,1,3,0:T(8,128)(2,1)S(1)}, bf16[1,16,128,130]{2,1,3,0:T(8,128)(2,1)S(1)}, u32[]{:S(2)}, u32[]{:S(2)}) collective-permute-start(bf16[1,16,128,130]{2,1,3,0:T(8,128)(2,1)S(1)} %copy.79), channel_id=1, source_target_pairs={{0,8},{8,16},{16,24},{1,9},{9,17},{17,25},{2,10},{10,18},{18,26},{... | collective-permute-start | bytes 1597448 | tf_op jit(solution)/shard_map/ppermute | solution.py:12
  40.4 10.3 %collective-permute-start.3 = (bf16[3,1,128,130]{2,3,1,0:T(8,128)(2,1)}, bf16[3,1,128,130]{2,3,1,0:T(8,128)(2,1)}, u32[]{:S(2)}, u32[]{:S(2)}) collective-permute-start(bf16[3,1,128,130]{2,3,1,0:T(8,128)(2,1)} %copy.84), channel_id=1, source_target_pairs={{4,0},{5,1},{6,2},{7,3},{12,8},{13,9},{14,10},{15,11},{20,16},{21,... | collective-permute-start | bytes 299528 | tf_op jit(solution)/shard_map/ppermute | solution.py:15
  41.6 9.0 %collective-permute-start.2 = (bf16[3,1,128,130]{2,3,1,0:T(8,128)(2,1)S(1)}, bf16[3,1,128,130]{2,3,1,0:T(8,128)(2,1)}, u32[]{:S(2)}, u32[]{:S(2)}) collective-permute-start(bf16[3,1,128,130]{2,3,1,0:T(8,128)(2,1)S(1)} %copy.83), channel_id=1, source_target_pairs={{0,4},{1,5},{2,6},{3,7},{8,12},{9,13},{10,14},{11,15},{16,20},{17,... | collective-permute-start | bytes 299528 | tf_op jit(solution)/shard_map/ppermute | solution.py:12
  57.1 0.7 copy-start.6
  62.3 0.7 copy-start.3
  78.5 13.7 %copy-start.2 = (bf16[1,16,128,130]{3,1,0,2:T(8,128)(2,1)}, bf16[1,16,128,130]{3,1,0,2:T(8,128)(2,1)S(1)}, u32[]{:S(2)}) copy-start(bf16[1,16,128,130]{3,1,0,2:T(8,128)(2,1)S(1)} %pad.8) | copy-start | bytes 1597444
  79.7 8.7 %collective-permute-start.5 = (bf16[1,16,128,130]{2,1,3,0:T(8,128)(2,1)S(1)}, bf16[1,16,128,130]{2,1,3,0:T(8,128)(2,1)S(1)}, u32[]{:S(2)}, u32[]{:S(2)}) collective-permute-start(bf16[1,16,128,130]{2,1,3,0:T(8,128)(2,1)S(1)} %copy.91), channel_id=1, source_target_pairs={{8,0},{16,8},{24,16},{9,1},{17,9},{25,17},{10,2},{18,10},{26,18},{... | collective-permute-start | bytes 1597448 | tf_op jit(solution)/shard_map/ppermute | solution.py:15
  81.6 10.6 %collective-permute-start.4 = (bf16[1,16,128,130]{2,1,3,0:T(8,128)(2,1)S(1)}, bf16[1,16,128,130]{2,1,3,0:T(8,128)(2,1)S(1)}, u32[]{:S(2)}, u32[]{:S(2)}) collective-permute-start(bf16[1,16,128,130]{2,1,3,0:T(8,128)(2,1)S(1)} %copy.91), channel_id=1, source_target_pairs={{0,8},{8,16},{16,24},{1,9},{9,17},{17,25},{2,10},{10,18},{18,26},{... | collective-permute-start | bytes 1597448 | tf_op jit(solution)/shard_map/ppermute | solution.py:12
  98.0 8.4 %collective-permute-start.6 = (bf16[3,1,128,130]{3,1,0,2:T(2,128)(2,1)}, bf16[3,1,128,130]{3,1,0,2:T(2,128)(2,1)}, u32[]{:S(2)}, u32[]{:S(2)}) collective-permute-start(bf16[3,1,128,130]{3,1,0,2:T(2,128)(2,1)} %get-tuple-element.5), channel_id=1, source_target_pairs={{0,4},{1,5},{2,6},{3,7},{8,12},{9,13},{10,14},{11,15},{16,20},{17,... | collective-permute-start | bytes 299528 | tf_op jit(solution)/shard_map/ppermute | solution.py:12
  101.6 10.0 %collective-permute-start.7 = (bf16[3,1,128,130]{3,1,0,2:T(2,128)(2,1)}, bf16[3,1,128,130]{3,1,0,2:T(2,128)(2,1)}, u32[]{:S(2)}, u32[]{:S(2)}) collective-permute-start(bf16[3,1,128,130]{3,1,0,2:T(2,128)(2,1)} %get-tuple-element.6), channel_id=1, source_target_pairs={{4,0},{5,1},{6,2},{7,3},{12,8},{13,9},{14,10},{15,11},{20,16},{21,... | collective-permute-start | bytes 299528 | tf_op jit(solution)/shard_map/ppermute | solution.py:15
  119.2 0.9 copy-start.5
  124.6 0.7 copy-start.4
where the time goes:
time: 127 us; the launch traced here: 126 us
  local copies, waits for them, and re-layouts  39.1 us (31%)
  blocking collectives  31.4 us (25%)
  starting transfers between devices  20.9 us (16%)
  waiting for transfers between devices  16.7 us (13%)
  other arithmetic  9.15 us (7%)
  matrix products  8.49 us (7%)
    all_gather x2, blocking collectives, layer_channels(): whole = lax.all_gather(field, 'ch', axis=2, tiled=True)  31.4 us
    ppermute x4, starting transfers between devices, with_halo(): lax.ppermute(lax.slice_in_dim(block, block.shape[dim] - width, None, axis...  14.5 us
    ppermute x4, waiting for transfers between devices, with_halo(): lax.ppermute(lax.slice_in_dim(block, 0, width, axis=dim), axis, backward)  12.4 us
    conv_general_dilated x2, matrix products, conv_taps(): lax.conv_general_dilated(padded[None], kernel, (1, 1, 1), 'VALID', dimens...  8.49 us
    conv_general_dilated x10, local copies, waits for them, and re-layouts, conv_taps(): lax.conv_general_dilated(padded[None], kernel, (1, 1, 1), 'VALID', dimens...  7.88 us
    ppermute x4, starting transfers between devices, with_halo(): lax.ppermute(lax.slice_in_dim(block, 0, width, axis=dim), axis, backward)  6.4 us
    concatenate x2, local copies, waits for them, and re-layouts, with_halo(): block = jnp.concatenate([low, block, high], axis=dim)  6.33 us
    ppermute x3, local copies, waits for them, and re-layouts, with_halo(): lax.ppermute(lax.slice_in_dim(block, block.shape[dim] - width, None, axis...  4.91 us
  transfers between devices with their start and end apart: 8, of which 6 were waited for; matrix products, arithmetic and copies ran while one was open for 9% of the time, Pallas kernels for 0%

commit v1 on v0

--- a/solution.py
+++ b/solution.py
@@ -1,7 +1,39 @@
+import functools
 import jax
 import jax.numpy as jnp
 from jax import lax
 from jax.sharding import PartitionSpec as P
+
+
+def bring_the_tokens(values, pos_dim):
+    values = jnp.moveaxis(values, 0, pos_dim)
+    y = values.shape
+    return values.reshape(*y[:pos_dim], y[pos_dim] * y[pos_dim + 1], *y[pos_dim + 2 :])
+
+
+def recover_signs(x_in, link_axis, dim_at):
+    ndev = lax.axis_size(link_axis)
+    latest = range(ndev)
+    lower = map(lambda hop_no: (hop_no, (hop_no + 1) % ndev), latest)
+    by_rank = list(lower)
+    lanes = [(s, k0) for k0, s in by_rank]
+    built, local_next = ([], [])
+    for dev in range(ndev - 1):
+        if dev % 2 == 0:
+            v_next = lax.ppermute(built[-1] if built else x_in, link_axis, by_rank)
+            built.append(v_next)
+        else:
+            near = lax.ppermute(local_next[-1] if local_next else x_in, link_axis, lanes)
+            local_next.append(near)
+    big = jnp.stack([*built[::-1], x_in, *local_next])
+    met_up = lax.axis_index(link_axis)
+    taken_in = len(built)
+    a_now = met_up - taken_in
+    big = big[(jnp.arange(ndev) - a_now) % ndev]
+    return bring_the_tokens(big, dim_at)
+
+
+balance_spans = functools.partial(recover_signs, link_axis="ch", dim_at=2)
 
 
 def with_halo(block, sides, width):
@@ -38,7 +70,7 @@
 
 
 def layer_channels(field, kernel, bias):
-    whole = lax.all_gather(field, "ch", axis=2, tiled=True)
+    whole = balance_spans(field)
     padded = with_halo(pad_depth(whole), (("gx", 0), ("gy", 1)), 1)
     total = conv_taps(padded, kernel)
     return finish(total, bias)

time: 127 us -> 117 us (0.921)
  the two profiles are of different devices: /device:TPU:12 before, /device:TPU:4 now
where the time goes in v1:
time: 117 us
  waiting for transfers between devices  48 us (41%)
  local copies, waits for them, and re-layouts  28.7 us (25%)
  starting transfers between devices  24.1 us (21%)
  matrix products  8.49 us (7%)
  other arithmetic  6.7 us (6%)
    ppermute x4, waiting for transfers between devices, recover_signs(): v_next = lax.ppermute(built[-1] if built else x_in, link_axis, by_rank)  19.3 us
    ppermute x4, waiting for transfers between devices, with_halo(): lax.ppermute(lax.slice_in_dim(block, 0, width, axis=dim), axis, backward)  17.5 us
    ppermute x4, waiting for transfers between devices, with_halo(): lax.ppermute(lax.slice_in_dim(block, block.shape[dim] - width, None, axis...  10.2 us
    unnamed x14, local copies, waits for them, and re-layouts  9.85 us
    ppermute x4, starting transfers between devices, with_halo(): lax.ppermute(lax.slice_in_dim(block, block.shape[dim] - width, None, axis...  9.85 us
    conv_general_dilated x2, matrix products, conv_taps(): lax.conv_general_dilated(padded[None], kernel, (1, 1, 1), 'VALID', dimens...  8.49 us
    conv_general_dilated x10, local copies, waits for them, and re-layouts, conv_taps(): lax.conv_general_dilated(padded[None], kernel, (1, 1, 1), 'VALID', dimens...  7.88 us
    ppermute x4, starting transfers between devices, with_halo(): lax.ppermute(lax.slice_in_dim(block, 0, width, axis=dim), axis, backward)  6.61 us
  transfers between devices with their start and end apart: 14, of which 13 were waited for; matrix products, arithmetic and copies ran while one was open for 2% of the time, Pallas kernels for 0%

profile of v1, /device:TPU:4, one launch (start us, length us, event | category | flops | bytes accessed | tf_op | source)
XLA Modules:
  0.0 116.5 jit_solution(18308567674322929433)
XLA Ops:
  0.0 1.6 %collective-permute-start = (bf16[1,16,32,128]{3,2,1,0:T(8,128)(2,1)}, bf16[1,16,32,128]{3,2,1,0:T(8,128)(2,1)S(1)}, u32[]{:S(2)}, u32[]{:S(2)}) collective-permute-start(bf16[1,16,32,128]{3,2,1,0:T(8,128)(2,1)} %param.5), channel_id=1, source_target_pairs={{0,1},{1,2},{2,3},{3,0},{4,5},{5,6},{6,7},{7,4},{8,9},{9,10},{10,1... | collective-permute-start | bytes 393224 | tf_op jit(solution)/shard_map/ppermute | solution.py:23
  1.6 2.2 %collective-permute-start.2 = (bf16[1,16,32,128]{3,2,1,0:T(8,128)(2,1)}, bf16[1,16,32,128]{3,2,1,0:T(8,128)(2,1)S(1)}, u32[]{:S(2)}, u32[]{:S(2)}) collective-permute-start(bf16[1,16,32,128]{3,2,1,0:T(8,128)(2,1)} %param.5), channel_id=1, source_target_pairs={{1,0},{2,1},{3,2},{0,3},{5,4},{6,5},{7,6},{4,7},{9,8},{10,9},{11,1... | collective-permute-start | bytes 393224 | tf_op jit(solution)/shard_map/ppermute | solution.py:26
  3.8 4.6 %collective-permute-done = bf16[1,16,32,128]{3,2,1,0:T(8,128)(2,1)S(1)} collective-permute-done((bf16[1,16,32,128]{3,2,1,0:T(8,128)(2,1)}, bf16[1,16,32,128]{3,2,1,0:T(8,128)(2,1)S(1)}, u32[]{:S(2)}, u32[]{:S(2)}) %collective-permute-start) | collective-permute-done | bytes 131104 | tf_op jit(solution)/shard_map/ppermute | solution.py:23
  8.4 1.1 collective-permute-done.2
  9.6 5.6 %collective-permute-done.1 = bf16[1,16,32,128]{3,2,1,0:T(8,128)(2,1)S(1)} collective-permute-done((bf16[1,16,32,128]{3,2,1,0:T(8,128)(2,1)S(1)}, bf16[1,16,32,128]{3,2,1,0:T(8,128)(2,1)S(1)}, u32[]{:S(2)}, u32[]{:S(2)}) %collective-permute-start.1) | collective-permute-done | bytes 131104 | tf_op jit(solution)/shard_map/ppermute | solution.py:23
  15.2 1.0 maximum_bitcast_fusion.2
  16.1 0.6 gather_fusion
  16.8 0.4 pad.7
  17.2 0.7 copy.87
  17.9 1.9 %collective-permute-start.4 = (bf16[1,16,128,130]{2,1,3,0:T(8,128)(2,1)S(1)}, bf16[1,16,128,130]{2,1,3,0:T(8,128)(2,1)S(1)}, u32[]{:S(2)}, u32[]{:S(2)}) collective-permute-start(bf16[1,16,128,130]{2,1,3,0:T(8,128)(2,1)S(1)} %copy.87), channel_id=1, source_target_pairs={{8,0},{16,8},{24,16},{9,1},{17,9},{25,17},{10,2},{18,10},{26,18},{... | collective-permute-start | bytes 1597448 | tf_op jit(solution)/shard_map/ppermute | solution.py:47
  19.8 2.4 %collective-permute-start.3 = (bf16[1,16,128,130]{2,1,3,0:T(8,128)(2,1)S(1)}, bf16[1,16,128,130]{2,1,3,0:T(8,128)(2,1)}, u32[]{:S(2)}, u32[]{:S(2)}) collective-permute-start(bf16[1,16,128,130]{2,1,3,0:T(8,128)(2,1)S(1)} %copy.87), channel_id=1, source_target_pairs={{0,8},{8,16},{16,24},{1,9},{9,17},{17,25},{2,10},{10,18},{18,26},{... | collective-permute-start | bytes 1597448 | tf_op jit(solution)/shard_map/ppermute | solution.py:44
  22.3 4.3 %collective-permute-done.4 = bf16[1,16,128,130]{2,1,3,0:T(8,128)(2,1)S(1)} collective-permute-done((bf16[1,16,128,130]{2,1,3,0:T(8,128)(2,1)S(1)}, bf16[1,16,128,130]{2,1,3,0:T(8,128)(2,1)S(1)}, u32[]{:S(2)}, u32[]{:S(2)}) %collective-permute-start.4) | collective-permute-done | bytes 532512 | tf_op jit(solution)/shard_map/ppermute | solution.py:47
  26.6 0.6 copy.90
  27.2 3.3 %collective-permute-done.3 = bf16[1,16,128,130]{2,1,3,0:T(8,128)(2,1)} collective-permute-done((bf16[1,16,128,130]{2,1,3,0:T(8,128)(2,1)S(1)}, bf16[1,16,128,130]{2,1,3,0:T(8,128)(2,1)}, u32[]{:S(2)}, u32[]{:S(2)}) %collective-permute-start.3) | collective-permute-done | bytes 532512 | tf_op jit(solution)/shard_map/ppermute | solution.py:44
  30.5 1.5 %copy.89 = bf16[1,16,128,130]{3,2,1,0:T(8,128)(2,1)S(1)} copy(bf16[1,16,128,130]{2,1,3,0:T(8,128)(2,1)} %collective-permute-done.3) | data formatting | bytes 1064960 | tf_op jit(solution)/shard_map/ppermute | solution.py:44
  32.0 0.1 pad_maximum_fusion.5
  32.1 3.4 %collective-permute-start.5 = (bf16[3,1,128,130]{3,2,1,0:T(8,128)(2,1)S(1)}, bf16[3,1,128,130]{3,2,1,0:T(8,128)(2,1)S(1)}, u32[]{:S(2)}, u32[]{:S(2)}) collective-permute-start(bf16[3,1,128,130]{3,2,1,0:T(8,128)(2,1)S(1)} %get-tuple-element.7), channel_id=1, source_target_pairs={{0,4},{1,5},{2,6},{3,7},{8,12},{9,13},{10,14},{11,15},{16,20},{17,... | collective-permute-start | bytes 299528 | tf_op jit(solution)/shard_map/ppermute | solution.py:44
  35.5 1.3 %collective-permute-start.6 = (bf16[3,1,128,130]{3,2,1,0:T(8,128)(2,1)S(1)}, bf16[3,1,128,130]{3,2,1,0:T(8,128)(2,1)S(1)}, u32[]{:S(2)}, u32[]{:S(2)}) collective-permute-start(bf16[3,1,128,130]{3,2,1,0:T(8,128)(2,1)S(1)} %get-tuple-element.8), channel_id=1, source_target_pairs={{4,0},{5,1},{6,2},{7,3},{12,8},{13,9},{14,10},{15,11},{20,16},{21,... | collective-permute-start | bytes 299528 | tf_op jit(solution)/shard_map/ppermute | solution.py:47
  36.8 1.9 %collective-permute-done.5 = bf16[3,1,128,130]{3,2,1,0:T(8,128)(2,1)S(1)} collective-permute-done((bf16[3,1,128,130]{3,2,1,0:T(8,128)(2,1)S(1)}, bf16[3,1,128,130]{3,2,1,0:T(8,128)(2,1)S(1)}, u32[]{:S(2)}, u32[]{:S(2)}) %collective-permute-start.5) | collective-permute-done | bytes 99872 | tf_op jit(solution)/shard_map/ppermute | solution.py:44
  38.7 4.4 %collective-permute-done.6 = bf16[3,1,128,130]{3,2,1,0:T(8,128)(2,1)S(1)} collective-permute-done((bf16[3,1,128,130]{3,2,1,0:T(8,128)(2,1)S(1)}, bf16[3,1,128,130]{3,2,1,0:T(8,128)(2,1)S(1)}, u32[]{:S(2)}, u32[]{:S(2)}) %collective-permute-start.6) | collective-permute-done | bytes 99872 | tf_op jit(solution)/shard_map/ppermute | solution.py:47
  43.1 2.3 %maximum_bitcast_fusion = bf16[3,18,128,1,130]{4,2,1,0,3:T(8,128)(2,1)} fusion(bf16[3,1,128,130]{3,2,1,0:T(8,128)(2,1)S(1)} %collective-permute-done.6, bf16[1,16,128,130]{3,2,1,0:T(8,128)(2,1)S(1)} %copy.90, bf16[1,16,128,130]{3,2,1,0:T(8,128)(2,1)S(1)} %pad.7, bf16[1,16,128,130]{3,2,1,0:T(8,128)(2,1)S(1)} %copy.89, ...), kind=kLoop, calls=%fused_computation.5 | loop fusion | flops 3594240 | bytes 3594240 | tf_op jit(solution)/shard_map/broadcast_in_dim | solution.py:54
  45.4 4.0 %copy.110 = bf16[3,18,128,1,130]{2,4,1,0,3:T(8,128)(2,1)S(1)} copy(bf16[3,18,128,1,130]{4,2,1,0,3:T(8,128)(2,1)} %maximum_bitcast_fusion) | data formatting | bytes 3594240
  49.4 1.4 %pad.9.clone = bf16[3,18,128,1,136]{2,4,1,0,3:T(8,128)(2,1)} pad(bf16[3,18,128,1,130]{2,4,1,0,3:T(8,128)(2,1)S(1)} %copy.110, bf16[]{:T(256)} %constant.30.clone.1), padding=0_0x0_0x0_0x0_0x0_6 | pad | bytes 3677186 | tf_op jit(solution)/shard_map/broadcast_in_dim | solution.py:54
  50.8 3.3 %reshape.107 = bf16[3,18,128,1,8,17]{2,5,4,1,0,3:T(8,128)(2,1)S(1)} reshape(bf16[3,18,128,1,136]{2,4,1,0,3:T(8,128)(2,1)} %pad.9.clone) | data formatting | bytes 3760128 | tf_op jit(solution)/shard_map/conv_general_dilated | solution.py:53
  54.1 0.3 copy.93
  54.4 0.1 slice.25
  54.5 0.3 copy-done.1
  54.8 4.2 %maximum_convert_fusion = (bf16[1,16,8,17,32]{4,2,3,1,0:T(8,128)(2,1)S(1)}, f32[1,16,8,17,32]{4,2,3,1,0:T(8,128)S(1)}) fusion(f32[32]{0:T(128)S(1)} %copy-done.1, bf16[3,3,3,32,128]{4,3,2,1,0:T(8,128)(2,1)S(1)} %copy-done, bf16[3,18,128,1,7,2]{2,4,5,1,0,3:T(8,128)(2,1)S(1)} %slice.25, bf16[3,18,128,1,8,17]{2,4,5,1,0,3:T(8,128)(2,1)S(1)} %copy.93, ...), kind=kOutput, calls=%fused_computation.21 | convolution fusion | flops 487878656 | bytes 2712840 | tf_op jit(solution)/shard_map/conv_general_dilated | solution.py:53
  59.1 0.2 copy.94
  59.3 0.1 slice.26
  59.4 0.4 copy.108
  59.8 0.1 fusion.27
  59.9 3.8 %collective-permute-start.9 = (bf16[1,16,32,128]{3,2,1,0:T(8,128)(2,1)S(1)}, bf16[1,16,32,128]{3,2,1,0:T(8,128)(2,1)S(1)}, u32[]{:S(2)}, u32[]{:S(2)}) collective-permute-start(bf16[1,16,32,128]{3,2,1,0:T(8,128)(2,1)S(1)} %fusion.27), channel_id=1, source_target_pairs={{1,0},{2,1},{3,2},{0,3},{5,4},{6,5},{7,6},{4,7},{9,8},{10,9},{11,1... | collective-permute-start | bytes 393224 | tf_op jit(solution)/shard_map/ppermute | solution.py:26
  63.8 0.1 copy.96
  63.8 2.9 %collective-permute-done.7 = bf16[1,16,32,128]{3,2,1,0:T(8,128)(2,1)S(1)} collective-permute-done((bf16[1,16,32,128]{3,2,1,0:T(8,128)(2,1)S(1)}, bf16[1,16,32,128]{3,2,1,0:T(8,128)(2,1)S(1)}, u32[]{:S(2)}, u32[]{:S(2)}) %collective-permute-start.7) | collective-permute-done | bytes 131104 | tf_op jit(solution)/shard_map/ppermute | solution.py:23
  66.7 0.4 copy.97
  67.2 6.3 %collective-permute-done.8 = bf16[1,16,32,128]{3,2,1,0:T(8,128)(2,1)S(1)} collective-permute-done((bf16[1,16,32,128]{3,2,1,0:T(8,128)(2,1)S(1)}, bf16[1,16,32,128]{3,2,1,0:T(8,128)(2,1)S(1)}, u32[]{:S(2)}, u32[]{:S(2)}) %collective-permute-start.8) | collective-permute-done | bytes 131104 | tf_op jit(solution)/shard_map/ppermute | solution.py:23
  73.5 0.1 maximum_bitcast_fusion.3
  73.5 0.6 gather_fusion.1
  74.3 0.4 pad.8
  74.6 0.7 copy.99
  75.3 1.9 %collective-permute-start.11 = (bf16[1,16,128,130]{2,1,3,0:T(8,128)(2,1)S(1)}, bf16[1,16,128,130]{2,1,3,0:T(8,128)(2,1)S(1)}, u32[]{:S(2)}, u32[]{:S(2)}) collective-permute-start(bf16[1,16,128,130]{2,1,3,0:T(8,128)(2,1)S(1)} %copy.99), channel_id=1, source_target_pairs={{8,0},{16,8},{24,16},{9,1},{17,9},{25,17},{10,2},{18,10},{26,18},{... | collective-permute-start | bytes 1597448 | tf_op jit(solution)/shard_map/ppermute | solution.py:47
  77.2 2.4 %collective-permute-start.10 = (bf16[1,16,128,130]{2,1,3,0:T(8,128)(2,1)S(1)}, bf16[1,16,128,130]{2,1,3,0:T(8,128)(2,1)}, u32[]{:S(2)}, u32[]{:S(2)}) collective-permute-start(bf16[1,16,128,130]{2,1,3,0:T(8,128)(2,1)S(1)} %copy.99), channel_id=1, source_target_pairs={{0,8},{8,16},{16,24},{1,9},{9,17},{17,25},{2,10},{10,18},{18,26},{... | collective-permute-start | bytes 1597448 | tf_op jit(solution)/shard_map/ppermute | solution.py:44
  79.7 4.3 %collective-permute-done.11 = bf16[1,16,128,130]{2,1,3,0:T(8,128)(2,1)S(1)} collective-permute-done((bf16[1,16,128,130]{2,1,3,0:T(8,128)(2,1)S(1)}, bf16[1,16,128,130]{2,1,3,0:T(8,128)(2,1)S(1)}, u32[]{:S(2)}, u32[]{:S(2)}) %collective-permute-start.11) | collective-permute-done | bytes 532512 | tf_op jit(solution)/shard_map/ppermute | solution.py:47
  84.0 0.6 copy.102
  84.6 3.3 %collective-permute-done.10 = bf16[1,16,128,130]{2,1,3,0:T(8,128)(2,1)} collective-permute-done((bf16[1,16,128,130]{2,1,3,0:T(8,128)(2,1)S(1)}, bf16[1,16,128,130]{2,1,3,0:T(8,128)(2,1)}, u32[]{:S(2)}, u32[]{:S(2)}) %collective-permute-start.10) | collective-permute-done | bytes 532512 | tf_op jit(solution)/shard_map/ppermute | solution.py:44
  87.9 1.5 %copy.101 = bf16[1,16,128,130]{3,2,1,0:T(8,128)(2,1)S(1)} copy(bf16[1,16,128,130]{2,1,3,0:T(8,128)(2,1)} %collective-permute-done.10) | data formatting | bytes 1064960 | tf_op jit(solution)/shard_map/ppermute | solution.py:44
  89.4 0.1 pad_maximum_fusion.2
  89.5 1.6 %collective-permute-start.12 = (bf16[3,1,128,130]{3,2,1,0:T(8,128)(2,1)S(1)}, bf16[3,1,128,130]{3,2,1,0:T(8,128)(2,1)S(1)}, u32[]{:S(2)}, u32[]{:S(2)}) collective-permute-start(bf16[3,1,128,130]{3,2,1,0:T(8,128)(2,1)S(1)} %get-tuple-element.5), channel_id=1, source_target_pairs={{0,4},{1,5},{2,6},{3,7},{8,12},{9,13},{10,14},{11,15},{16,20},{17,... | collective-permute-start | bytes 299528 | tf_op jit(solution)/shard_map/ppermute | solution.py:44
  91.1 1.5 %collective-permute-start.13 = (bf16[3,1,128,130]{3,2,1,0:T(8,128)(2,1)S(1)}, bf16[3,1,128,130]{3,2,1,0:T(8,128)(2,1)S(1)}, u32[]{:S(2)}, u32[]{:S(2)}) collective-permute-start(bf16[3,1,128,130]{3,2,1,0:T(8,128)(2,1)S(1)} %get-tuple-element.6), channel_id=1, source_target_pairs={{4,0},{5,1},{6,2},{7,3},{12,8},{13,9},{14,10},{15,11},{20,16},{21,... | collective-permute-start | bytes 299528 | tf_op jit(solution)/shard_map/ppermute | solution.py:47
  92.6 1.7 %collective-permute-done.12 = bf16[3,1,128,130]{3,2,1,0:T(8,128)(2,1)S(1)} collective-permute-done((bf16[3,1,128,130]{3,2,1,0:T(8,128)(2,1)S(1)}, bf16[3,1,128,130]{3,2,1,0:T(8,128)(2,1)S(1)}, u32[]{:S(2)}, u32[]{:S(2)}) %collective-permute-start.12) | collective-permute-done | bytes 99872 | tf_op jit(solution)/shard_map/ppermute | solution.py:44
  94.2 4.4 %collective-permute-done.13 = bf16[3,1,128,130]{3,2,1,0:T(8,128)(2,1)S(1)} collective-permute-done((bf16[3,1,128,130]{3,2,1,0:T(8,128)(2,1)S(1)}, bf16[3,1,128,130]{3,2,1,0:T(8,128)(2,1)S(1)}, u32[]{:S(2)}, u32[]{:S(2)}) %collective-permute-start.13) | collective-permute-done | bytes 99872 | tf_op jit(solution)/shard_map/ppermute | solution.py:47
  98.6 2.3 %maximum_bitcast_fusion.1 = bf16[3,18,128,1,130]{4,2,1,0,3:T(8,128)(2,1)} fusion(bf16[3,1,128,130]{3,2,1,0:T(8,128)(2,1)S(1)} %collective-permute-done.13, bf16[1,16,128,130]{3,2,1,0:T(8,128)(2,1)S(1)} %copy.102, bf16[1,16,128,130]{3,2,1,0:T(8,128)(2,1)S(1)} %pad.8, bf16[1,16,128,130]{3,2,1,0:T(8,128)(2,1)S(1)} %copy.101, ...), kind=kLoop, calls=%fused_computation.6 | loop fusion | flops 3594240 | bytes 3594240 | tf_op jit(solution)/shard_map/broadcast_in_dim | solution.py:54
  100.9 4.0 %copy.111 = bf16[3,18,128,1,130]{2,4,1,0,3:T(8,128)(2,1)S(1)} copy(bf16[3,18,128,1,130]{4,2,1,0,3:T(8,128)(2,1)} %maximum_bitcast_fusion.1) | data formatting | bytes 3594240
  104.9 1.4 %pad.11.clone = bf16[3,18,128,1,136]{2,4,1,0,3:T(8,128)(2,1)} pad(bf16[3,18,128,1,130]{2,4,1,0,3:T(8,128)(2,1)S(1)} %copy.111, bf16[]{:T(256)} %constant.30.clone.1), padding=0_0x0_0x0_0x0_0x0_6 | pad | bytes 3677186 | tf_op jit(solution)/shard_map/broadcast_in_dim | solution.py:54
  106.3 3.3 %reshape.116 = bf16[3,18,128,1,8,17]{2,5,4,1,0,3:T(8,128)(2,1)S(1)} reshape(bf16[3,18,128,1,136]{2,4,1,0,3:T(8,128)(2,1)} %pad.11.clone) | data formatting | bytes 3760128 | tf_op jit(solution)/shard_map/conv_general_dilated | solution.py:53
  109.7 0.3 copy.105
  110.0 0.6 copy-done.3
  110.6 4.2 %fusion.16 = f32[1,16,8,17,32]{4,2,3,1,0:T(8,128)S(1)} fusion(bf16[3,3,3,32,128]{4,3,2,1,0:T(8,128)(2,1)S(1)} %copy-done.3, bf16[3,18,128,1,7,2]{2,4,5,1,0,3:T(8,128)(2,1)S(1)} %slice.28, bf16[3,18,128,1,8,17]{2,4,5,1,0,3:T(8,128)(2,1)S(1)} %copy.105, pred[8,17]{0,1:T(8,128)(4,1)S(1)} %copy-done.4), kind=kOutput, calls=%fused_computation.19 | convolution fusion | flops 487669760 | bytes 2573448 | tf_op jit(solution)/shard_map/conv_general_dilated | solution.py:53
  114.9 0.2 copy.106
  115.1 0.1 slice.29
  115.2 0.4 copy.109
  115.6 0.2 copy-done.2
  115.8 0.8 fusion.25
  (17 shorter events, 0.3 us)
Async XLA Ops:
  0.0 54.5 %copy-start = (bf16[3,3,3,32,128]{4,3,2,1,0:T(8,128)(2,1)S(1)}, bf16[3,3,3,32,128]{4,3,2,1,0:T(8,128)(2,1)}, u32[]{:S(2)}) copy-start(bf16[3,3,3,32,128]{4,3,2,1,0:T(8,128)(2,1)} %param.6) | copy-start | bytes 663556
  0.0 8.4 %collective-permute-start = (bf16[1,16,32,128]{3,2,1,0:T(8,128)(2,1)}, bf16[1,16,32,128]{3,2,1,0:T(8,128)(2,1)S(1)}, u32[]{:S(2)}, u32[]{:S(2)}) collective-permute-start(bf16[1,16,32,128]{3,2,1,0:T(8,128)(2,1)} %param.5), channel_id=1, source_target_pairs={{0,1},{1,2},{2,3},{3,0},{4,5},{5,6},{6,7},{7,4},{8,9},{9,10},{10,1... | collective-permute-start | bytes 393224 | tf_op jit(solution)/shard_map/ppermute | solution.py:23
  1.6 8.0 %collective-permute-start.2 = (bf16[1,16,32,128]{3,2,1,0:T(8,128)(2,1)}, bf16[1,16,32,128]{3,2,1,0:T(8,128)(2,1)S(1)}, u32[]{:S(2)}, u32[]{:S(2)}) collective-permute-start(bf16[1,16,32,128]{3,2,1,0:T(8,128)(2,1)} %param.5), channel_id=1, source_target_pairs={{1,0},{2,1},{3,2},{0,3},{5,4},{6,5},{7,6},{4,7},{9,8},{10,9},{11,1... | collective-permute-start | bytes 393224 | tf_op jit(solution)/shard_map/ppermute | solution.py:26
  8.4 6.8 %collective-permute-start.1 = (bf16[1,16,32,128]{3,2,1,0:T(8,128)(2,1)S(1)}, bf16[1,16,32,128]{3,2,1,0:T(8,128)(2,1)S(1)}, u32[]{:S(2)}, u32[]{:S(2)}) collective-permute-start(bf16[1,16,32,128]{3,2,1,0:T(8,128)(2,1)S(1)} %collective-permute-done), channel_id=1, source_target_pairs={{0,1},{1,2},{2,3},{3,0},{4,5},{5,6},{6,7},{7,4},{8,9},{9,10},{10,1... | collective-permute-start | bytes 393224 | tf_op jit(solution)/shard_map/ppermute | solution.py:23
  17.9 8.7 %collective-permute-start.4 = (bf16[1,16,128,130]{2,1,3,0:T(8,128)(2,1)S(1)}, bf16[1,16,128,130]{2,1,3,0:T(8,128)(2,1)S(1)}, u32[]{:S(2)}, u32[]{:S(2)}) collective-permute-start(bf16[1,16,128,130]{2,1,3,0:T(8,128)(2,1)S(1)} %copy.87), channel_id=1, source_target_pairs={{8,0},{16,8},{24,16},{9,1},{17,9},{25,17},{10,2},{18,10},{26,18},{... | collective-permute-start | bytes 1597448 | tf_op jit(solution)/shard_map/ppermute | solution.py:47
  19.8 10.7 %collective-permute-start.3 = (bf16[1,16,128,130]{2,1,3,0:T(8,128)(2,1)S(1)}, bf16[1,16,128,130]{2,1,3,0:T(8,128)(2,1)}, u32[]{:S(2)}, u32[]{:S(2)}) collective-permute-start(bf16[1,16,128,130]{2,1,3,0:T(8,128)(2,1)S(1)} %copy.87), channel_id=1, source_target_pairs={{0,8},{8,16},{16,24},{1,9},{9,17},{17,25},{2,10},{10,18},{18,26},{... | collective-permute-start | bytes 1597448 | tf_op jit(solution)/shard_map/ppermute | solution.py:44
  32.1 6.6 %collective-permute-start.5 = (bf16[3,1,128,130]{3,2,1,0:T(8,128)(2,1)S(1)}, bf16[3,1,128,130]{3,2,1,0:T(8,128)(2,1)S(1)}, u32[]{:S(2)}, u32[]{:S(2)}) collective-permute-start(bf16[3,1,128,130]{3,2,1,0:T(8,128)(2,1)S(1)} %get-tuple-element.7), channel_id=1, source_target_pairs={{0,4},{1,5},{2,6},{3,7},{8,12},{9,13},{10,14},{11,15},{16,20},{17,... | collective-permute-start | bytes 299528 | tf_op jit(solution)/shard_map/ppermute | solution.py:44
  35.5 7.6 %collective-permute-start.6 = (bf16[3,1,128,130]{3,2,1,0:T(8,128)(2,1)S(1)}, bf16[3,1,128,130]{3,2,1,0:T(8,128)(2,1)S(1)}, u32[]{:S(2)}, u32[]{:S(2)}) collective-permute-start(bf16[3,1,128,130]{3,2,1,0:T(8,128)(2,1)S(1)} %get-tuple-element.8), channel_id=1, source_target_pairs={{4,0},{5,1},{6,2},{7,3},{12,8},{13,9},{14,10},{15,11},{20,16},{21,... | collective-permute-start | bytes 299528 | tf_op jit(solution)/shard_map/ppermute | solution.py:47
  54.1 0.7 copy-start.1
  54.1 0.7 copy-start.4
  59.9 6.8 %collective-permute-start.7 = (bf16[1,16,32,128]{3,2,1,0:T(8,128)(2,1)S(1)}, bf16[1,16,32,128]{3,2,1,0:T(8,128)(2,1)S(1)}, u32[]{:S(2)}, u32[]{:S(2)}) collective-permute-start(bf16[1,16,32,128]{3,2,1,0:T(8,128)(2,1)S(1)} %fusion.27), channel_id=1, source_target_pairs={{0,1},{1,2},{2,3},{3,0},{4,5},{5,6},{6,7},{7,4},{8,9},{9,10},{10,1... | collective-permute-start | bytes 393224 | tf_op jit(solution)/shard_map/ppermute | solution.py:23
  59.9 7.2 %collective-permute-start.9 = (bf16[1,16,32,128]{3,2,1,0:T(8,128)(2,1)S(1)}, bf16[1,16,32,128]{3,2,1,0:T(8,128)(2,1)S(1)}, u32[]{:S(2)}, u32[]{:S(2)}) collective-permute-start(bf16[1,16,32,128]{3,2,1,0:T(8,128)(2,1)S(1)} %fusion.27), channel_id=1, source_target_pairs={{1,0},{2,1},{3,2},{0,3},{5,4},{6,5},{7,6},{4,7},{9,8},{10,9},{11,1... | collective-permute-start | bytes 393224 | tf_op jit(solution)/shard_map/ppermute | solution.py:26
  66.7 6.8 %collective-permute-start.8 = (bf16[1,16,32,128]{3,2,1,0:T(8,128)(2,1)S(1)}, bf16[1,16,32,128]{3,2,1,0:T(8,128)(2,1)S(1)}, u32[]{:S(2)}, u32[]{:S(2)}) collective-permute-start(bf16[1,16,32,128]{3,2,1,0:T(8,128)(2,1)S(1)} %collective-permute-done.7), channel_id=1, source_target_pairs={{0,1},{1,2},{2,3},{3,0},{4,5},{5,6},{6,7},{7,4},{8,9},{9,10},{10,1... | collective-permute-start | bytes 393224 | tf_op jit(solution)/shard_map/ppermute | solution.py:23
  75.3 8.7 %collective-permute-start.11 = (bf16[1,16,128,130]{2,1,3,0:T(8,128)(2,1)S(1)}, bf16[1,16,128,130]{2,1,3,0:T(8,128)(2,1)S(1)}, u32[]{:S(2)}, u32[]{:S(2)}) collective-permute-start(bf16[1,16,128,130]{2,1,3,0:T(8,128)(2,1)S(1)} %copy.99), channel_id=1, source_target_pairs={{8,0},{16,8},{24,16},{9,1},{17,9},{25,17},{10,2},{18,10},{26,18},{... | collective-permute-start | bytes 1597448 | tf_op jit(solution)/shard_map/ppermute | solution.py:47
  77.2 10.7 %collective-permute-start.10 = (bf16[1,16,128,130]{2,1,3,0:T(8,128)(2,1)S(1)}, bf16[1,16,128,130]{2,1,3,0:T(8,128)(2,1)}, u32[]{:S(2)}, u32[]{:S(2)}) collective-permute-start(bf16[1,16,128,130]{2,1,3,0:T(8,128)(2,1)S(1)} %copy.99), channel_id=1, source_target_pairs={{0,8},{8,16},{16,24},{1,9},{9,17},{17,25},{2,10},{10,18},{18,26},{... | collective-permute-start | bytes 1597448 | tf_op jit(solution)/shard_map/ppermute | solution.py:44
  89.5 4.7 %collective-permute-start.12 = (bf16[3,1,128,130]{3,2,1,0:T(8,128)(2,1)S(1)}, bf16[3,1,128,130]{3,2,1,0:T(8,128)(2,1)S(1)}, u32[]{:S(2)}, u32[]{:S(2)}) collective-permute-start(bf16[3,1,128,130]{3,2,1,0:T(8,128)(2,1)S(1)} %get-tuple-element.5), channel_id=1, source_target_pairs={{0,4},{1,5},{2,6},{3,7},{8,12},{9,13},{10,14},{11,15},{16,20},{17,... | collective-permute-start | bytes 299528 | tf_op jit(solution)/shard_map/ppermute | solution.py:44
  91.1 7.6 %collective-permute-start.13 = (bf16[3,1,128,130]{3,2,1,0:T(8,128)(2,1)S(1)}, bf16[3,1,128,130]{3,2,1,0:T(8,128)(2,1)S(1)}, u32[]{:S(2)}, u32[]{:S(2)}) collective-permute-start(bf16[3,1,128,130]{3,2,1,0:T(8,128)(2,1)S(1)} %get-tuple-element.6), channel_id=1, source_target_pairs={{4,0},{5,1},{6,2},{7,3},{12,8},{13,9},{14,10},{15,11},{20,16},{21,... | collective-permute-start | bytes 299528 | tf_op jit(solution)/shard_map/ppermute | solution.py:47
  109.7 0.9 copy-start.3
  115.1 0.7 copy-start.2
